TPU v7x, 512 devices: a whole 4x8x8 slice. The times are simulated.
512 devices in a mesh: member: 2 (over core), fsdp: 256 (over y, x, z).
Axes of the slice: x: 4, y: 8, z: 8, core: 2. Of those that a mesh axis runs over, the one named last changes fastest.
Arguments:
- hidden: bfloat16 [2, 512, 2048], P('member', 'fsdp'), may hold values from -60 to 60
- gain: float32 [2, 2048], P('member'), may hold values from 0.5 to 1.5
- head: bfloat16 [2, 2048, 128256], P('member', None, 'fsdp'), may hold values from -0.397747564 to 0.397747564
- labels: int32 [512], replicated, may hold values from 0 to 128255
Outputs:
- token_loss: float32 [2, 512], P('member', 'fsdp')
- head_grad: bfloat16 [2, 2048, 128256], P('member', None, 'fsdp')
- hidden_grad: bfloat16 [2, 512, 2048], P('member', 'fsdp')
All inputs are finite; a program needn't handle non-finite values.
Results may differ from a plain program's by a relative error of at most 0.0049.
Values may be sent and summed in bfloat16 or wider, within the bound.
A program may use at most 64 MiB of HBM per device.

v0:
```python
import jax
import jax.numpy as jnp
from jax import lax
from jax.sharding import PartitionSpec as P

EPS = 1e-05
BETA = 0.5


def swapped(value, axis, bit):
    return lax.ppermute(value, axis, [(i, i ^ 1 << bit) for i in range(lax.axis_size(axis))])


def normalize(rows, gain_row):
    values = rows.astype(jnp.float32)
    inverse = lax.rsqrt(jnp.mean(values * values, axis=-1, keepdims=True) + EPS)
    return ((values * inverse * gain_row).astype(jnp.bfloat16), inverse)


def norm_back(rows, inverse, gain_row, upstream):
    values = rows.astype(jnp.float32)
    scaled = gain_row * upstream
    inner = jnp.mean(scaled * values, axis=-1, keepdims=True)
    return inverse * scaled - values * inverse**3 * inner


def body(hidden, gain, head, labels):
    own_rows = hidden[0]
    gain_row = gain[0]
    weights_local = head[0]
    tok_dev = own_rows.shape[0]
    vocab_dev = weights_local.shape[1]
    own_start = lax.axis_index("fsdp") * tok_dev
    vocab_start = lax.axis_index("fsdp") * vocab_dev
    normed_own, inverse_own = normalize(own_rows, gain_row)
    normed = lax.all_gather(normed_own, "fsdp", axis=0, tiled=True)
    token_count = normed.shape[0]
    logits = jnp.dot(normed, weights_local, preferred_element_type=jnp.float32)
    local_label = labels - vocab_start
    columns = lax.broadcasted_iota(jnp.int32, (1, vocab_dev), 1)
    onehot_mask = local_label[:, None] == columns
    picked_part = jnp.sum(jnp.where(onehot_mask, logits, 0.0), axis=-1)
    row_top = lax.pmax(jnp.max(logits, axis=-1), "fsdp")
    row_total, picked = lax.psum(
        (jnp.sum(jnp.exp(logits - row_top[:, None]), axis=-1), picked_part), "fsdp"
    )
    log_total = row_top + jnp.log(row_total)
    logprob = (logits - log_total[:, None]).astype(jnp.bfloat16)
    teacher = swapped(logprob, "member", 0)
    target = jnp.exp(teacher.astype(jnp.float32))
    student = jnp.exp(logits - log_total[:, None])
    dlogits = (
        ((1.0 + BETA) * student - onehot_mask.astype(jnp.float32) - BETA * target) / token_count
    ).astype(jnp.bfloat16)
    cross_part = jnp.sum(target * (log_total[:, None] - logits), axis=-1)
    head_grad = lax.dot_general(
        normed, dlogits, (((0,), (0,)), ((), ())), preferred_element_type=jnp.float32
    ).astype(jnp.bfloat16)
    cross_whole = lax.psum(cross_part, "fsdp")
    cross_own = lax.dynamic_slice_in_dim(cross_whole, own_start, tok_dev, 0)
    partial_up = lax.dot_general(
        dlogits, weights_local, (((1,), (1,)), ((), ())), preferred_element_type=jnp.float32
    )
    summed = lax.psum_scatter(partial_up, "fsdp", scatter_dimension=0, tiled=True)
    total_own = lax.dynamic_slice_in_dim(log_total, own_start, tok_dev, 0)
    picked_own = lax.dynamic_slice_in_dim(picked, own_start, tok_dev, 0)
    token_loss = total_own - picked_own + BETA * cross_own
    hidden_grad = norm_back(own_rows, inverse_own, gain_row, summed)
    return (token_loss[None], head_grad[None], hidden_grad.astype(jnp.bfloat16)[None])


def solution(mesh):
    in_specs = (P("member", "fsdp", None), P("member", None), P("member", None, "fsdp"), P())
    out_specs = (P("member", "fsdp"), P("member", None, "fsdp"), P("member", "fsdp", None))
    return jax.shard_map(body, mesh=mesh, in_specs=in_specs, out_specs=out_specs, check_vma=False)
```

profile of v0, /device:TPU:32, one launch (start us, length us, event | category | flops | bytes accessed | tf_op | source)
XLA Modules:
  0.0 2223.4 jit_solution(17684733254813426398)
XLA Ops:
  7.2 0.0 copy-start
  7.2 0.0 all-gather.3.cloned.1.call-start
  7.2 1.0 fusion.5
  8.2 1.4 fusion.12
  9.6 0.0 all-gather.3.cloned.1.call-update
  9.6 0.0 all-reduce.4.cloned.1.call-start
  9.7 121.9 %all-gather.3.cloned.1.call-done = bf16[256,2,2048]{2,1,0:T(2,128)(2,1)} async-done(((bf16[1,2,2048]{2,1,0:T(2,128)(2,1)}), bf16[256,2,2048]{2,1,0:T(2,128)(2,1)}) %all-gather.3.cloned.1.call-update) | async-done | bytes 2097168 | tf_op jit(solution)/shard_map/all_gather | solution.py:36
  131.6 4.1 reshape.31
  135.8 0.0 copy-done
  135.8 2.9 fusion.14
  138.6 0.0 copy-start.5
  138.7 688.6 %pmax.7 = f32[512]{0:T(512)S(1)} all-reduce(f32[512]{0:T(512)S(1)} %get-tuple-element.10), channel_id=1, replica_groups=mesh['member'=2,'fsdp'=256] {'fsdp'}, use_global_device_ids=true, to_apply=%region_2.3 | all-reduce | flops 512 | bytes 4096 | tf_op jit(solution)/shard_map/pmax | solution.py:43
  827.3 0.2 exponential_reduce_fusion
  827.5 683.0 %psum.21 = f32[512]{0:T(512)S(1)} all-reduce(f32[512]{0:T(512)S(1)} %exponential_reduce_fusion), channel_id=1, replica_groups=mesh['member'=2,'fsdp'=256] {'fsdp'}, use_global_device_ids=true, to_apply=%region_4.5 | all-reduce | flops 512 | bytes 4096 | tf_op jit(solution)/shard_map/psum | solution.py:44
  1510.5 0.9 subtract_convert_fusion
  1511.4 1.9 collective-permute-start
  1513.3 0.0 copy-done.5
  1513.3 2.2 collective-permute-done
  1515.5 1.7 select_reduce_fusion
  1517.2 0.0 copy-start.1
  1517.2 0.8 copy-done.1
  1518.0 3.3 fusion.1
  1521.3 0.0 all-reduce.4.cloned.1.call-update
  1521.3 1.3 dynamic-slice
  1523.3 686.0 %all-reduce.1 = (f32[512]{0:T(512)S(1)}, f32[512]{0:T(512)S(1)}) all-reduce(f32[512]{0:T(512)S(1)} %get-tuple-element.4, f32[512]{0:T(512)S(1)} %get-tuple-element.3), channel_id=1, replica_groups=mesh['member'=2,'fsdp'=256] {'fsdp'}, use_global_device_ids=true, to_apply=%region_8.9 | all-reduce | flops 1024 | bytes 8192 | tf_op jit(solution)/shard_map/psum | solution.py:59
  2209.3 0.6 add_bitcast_fusion
  2209.9 0.0 copy-done.2
  2209.9 4.2 fusion
  2214.0 0.0 copy-done.3
  2214.1 0.0 copy-done.4
  2214.1 1.0 fusion.11
  2215.0 1.5 fusion.13
  (8 shorter events, 0.0 us)
Async XLA Ops:
  7.2 128.6 %copy-start = (bf16[1,2048,501]{1,2,0:T(8,128)(2,1)S(1)}, bf16[1,2048,501]{1,2,0:T(8,128)(2,1)}, u32[]{:S(2)}) copy-start(bf16[1,2048,501]{1,2,0:T(8,128)(2,1)} %param.6) | copy-start | bytes 6156292
  7.2 124.4 %all-gather.3.cloned.1.call-start = ((), (), s32[]{:S(2)}) async-start(), calls=%async_computation | async-start | bytes 2105344 | tf_op jit(solution)/shard_map/all_gather | solution.py:36
  9.6 2204.4 %all-reduce.4.cloned.1.call-start = ((), (), s32[]{:S(2)}) async-start(), calls=%async_computation.1 | async-start | bytes 8388608
  138.6 1374.7 %copy-start.5 = (s32[512]{0:T(512)S(1)}, s32[512]{0:T(512)}, u32[]{:S(2)}) copy-start(s32[512]{0:T(512)} %param.7) | copy-start | bytes 6148
  1511.4 4.1 collective-permute-start
  1517.2 0.8 copy-start.1
  1521.3 688.6 %copy-start.2 = (bf16[512,501]{0,1:T(8,128)(2,1)S(1)}, bf16[512,501]{0,1:T(8,128)(2,1)}, u32[]{:S(2)}) copy-start(bf16[512,501]{0,1:T(8,128)(2,1)} %copy-done.1) | copy-start | bytes 1539076
  2209.9 4.2 copy-start.3
  2209.9 4.2 copy-start.4
Sparse Core Ops, SparseCore 0:
  12.6 118.9 all-gather.2
  1521.4 245.9 all-reduce.3
where the time goes:
time: 2220 us
  blocking collectives  2060 us (93%)
  waiting for transfers between devices  124 us (6%)
    pmax x1, blocking collectives, body(): row_top = lax.pmax(jnp.max(logits, axis=-1), 'fsdp')  689 us
    psum x1, blocking collectives, body(): cross_whole = lax.psum(cross_part, 'fsdp')  686 us
    psum x1, blocking collectives, body(): lax.psum((jnp.sum(jnp.exp(logits - row_top[:, None]), axis=-1), picked_pa...  683 us
    all_gather x1, waiting for transfers between devices, body(): normed = lax.all_gather(normed_own, 'fsdp', axis=0, tiled=True)  122 us
  transfers between devices with their start and end apart: 3, of which 2 were waited for; matrix products, arithmetic and copies ran while one was open for 0% of the time, Pallas kernels for 0%

commit v1 on v0

--- a/solution.py
+++ b/solution.py
@@ -5,6 +5,11 @@
 
 EPS = 1e-05
 BETA = 0.5
+
+
+def add_all(x, name):
+    parts = lax.all_gather(x, name)
+    return jnp.sum(parts, axis=0)
 
 
 def swapped(value, axis, bit):
@@ -56,7 +61,7 @@
     head_grad = lax.dot_general(
         normed, dlogits, (((0,), (0,)), ((), ())), preferred_element_type=jnp.float32
     ).astype(jnp.bfloat16)
-    cross_whole = lax.psum(cross_part, "fsdp")
+    cross_whole = add_all(cross_part, "fsdp")
     cross_own = lax.dynamic_slice_in_dim(cross_whole, own_start, tok_dev, 0)
     partial_up = lax.dot_general(
         dlogits, weights_local, (((1,), (1,)), ((), ())), preferred_element_type=jnp.float32

time: 2220 us -> 2900 us (1.31)
  the two profiles are of different devices: /device:TPU:32 before, /device:TPU:64 now
where the time goes in v1:
time: 2900 us
  blocking collectives  2740 us (94%)
  waiting for transfers between devices  125 us (4%)
    psum x2, blocking collectives, body(): lax.psum((jnp.sum(jnp.exp(logits - row_top[:, None]), axis=-1), picked_pa...  1370 us
    pmax x1, blocking collectives, body(): row_top = lax.pmax(jnp.max(logits, axis=-1), 'fsdp')  684 us
    all_gather x1, blocking collectives, add_all(): parts = lax.all_gather(x, name)  678 us
    all_gather x1, waiting for transfers between devices, body(): normed = lax.all_gather(normed_own, 'fsdp', axis=0, tiled=True)  123 us
  transfers between devices with their start and end apart: 3, of which 2 were waited for; matrix products, arithmetic and copies ran while one was open for 0% of the time, Pallas kernels for 0%

profile of v1, /device:TPU:64, one launch (start us, length us, event | category | flops | bytes accessed | tf_op | source)
XLA Modules:
  0.0 2902.6 jit_solution(10088482010253924896)
XLA Ops:
  7.2 0.0 copy-start
  7.2 0.0 all-gather.5.cloned.1.call-start
  7.2 1.0 fusion.5
  8.2 1.4 fusion.12
  9.6 0.0 all-gather.5.cloned.1.call-update
  9.6 0.0 all-reduce.3.cloned.1.call-start
  9.7 123.2 %all-gather.5.cloned.1.call-done = bf16[256,2,2048]{2,1,0:T(2,128)(2,1)} async-done(((bf16[1,2,2048]{2,1,0:T(2,128)(2,1)}), bf16[256,2,2048]{2,1,0:T(2,128)(2,1)}) %all-gather.5.cloned.1.call-update) | async-done | bytes 2097168 | tf_op jit(solution)/shard_map/all_gather | solution.py:41
  132.8 4.1 reshape.32
  137.0 0.0 copy-done
  137.0 2.9 fusion.14
  139.9 0.0 copy-start.5
  139.9 683.9 %pmax.7 = f32[512]{0:T(512)S(1)} all-reduce(f32[512]{0:T(512)S(1)} %get-tuple-element.8), channel_id=1, replica_groups=mesh['member'=2,'fsdp'=256] {'fsdp'}, use_global_device_ids=true, to_apply=%region_2.3 | all-reduce | flops 512 | bytes 4096 | tf_op jit(solution)/shard_map/pmax | solution.py:48
  823.8 0.2 exponential_reduce_fusion
  823.9 688.2 %psum.14 = f32[512]{0:T(512)S(1)} all-reduce(f32[512]{0:T(512)S(1)} %exponential_reduce_fusion), channel_id=1, replica_groups=mesh['member'=2,'fsdp'=256] {'fsdp'}, use_global_device_ids=true, to_apply=%region_4.5 | all-reduce | flops 512 | bytes 4096 | tf_op jit(solution)/shard_map/psum | solution.py:49
  1512.2 0.9 subtract_convert_fusion
  1513.1 1.9 collective-permute-start
  1515.0 0.0 copy-done.5
  1515.1 2.2 collective-permute-done
  1517.2 1.7 select_reduce_fusion
  1518.9 0.0 copy-start.1
  1519.0 0.8 copy-done.1
  1519.7 3.3 fusion.1
  1523.0 0.0 all-reduce.3.cloned.1.call-update
  1523.0 1.3 dynamic-slice
  1525.0 678.1 %all-gather.2 = f32[256,1,512]{2,1,0:T(1,128)S(1)} all-gather(f32[1,1,512]{2,1,0:T(1,128)S(1)} %bitcast.35), channel_id=2, replica_groups=mesh['member'=2,'fsdp'=256] {'fsdp'}, dimensions={0}, use_global_device_ids=true | all-gather | bytes 526336 | tf_op jit(solution)/shard_map/all_gather | solution.py:11
  2203.1 0.3 reduce_sum.58
  2203.4 685.0 %psum.15 = f32[512]{0:T(512)S(1)} all-reduce(f32[512]{0:T(512)S(1)} %get-tuple-element.3), channel_id=1, replica_groups=mesh['member'=2,'fsdp'=256] {'fsdp'}, use_global_device_ids=true, to_apply=%region_6.7 | all-reduce | flops 512 | bytes 4096 | tf_op jit(solution)/shard_map/psum | solution.py:49
  2888.5 0.6 add_bitcast_fusion
  2889.0 0.0 copy-done.2
  2889.1 4.2 fusion
  2893.2 1.0 fusion.11
  2894.2 1.5 fusion.13
  (10 shorter events, 0.0 us)
Async XLA Ops:
  7.2 129.8 %copy-start = (bf16[1,2048,501]{1,2,0:T(8,128)(2,1)S(1)}, bf16[1,2048,501]{1,2,0:T(8,128)(2,1)}, u32[]{:S(2)}) copy-start(bf16[1,2048,501]{1,2,0:T(8,128)(2,1)} %param.6) | copy-start | bytes 6156292
  7.2 125.7 %all-gather.5.cloned.1.call-start = ((), (), s32[]{:S(2)}) async-start(), calls=%async_computation | async-start | bytes 2105344 | tf_op jit(solution)/shard_map/all_gather | solution.py:41
  9.6 2883.6 %all-reduce.3.cloned.1.call-start = ((), (), s32[]{:S(2)}) async-start(), calls=%async_computation.1 | async-start | bytes 8388608
  139.9 1375.2 %copy-start.5 = (s32[512]{0:T(512)S(1)}, s32[512]{0:T(512)}, u32[]{:S(2)}) copy-start(s32[512]{0:T(512)} %param.7) | copy-start | bytes 6148
  1513.1 4.1 collective-permute-start
  1518.9 0.8 copy-start.1
  1523.0 1366.0 %copy-start.2 = (bf16[512,501]{0,1:T(8,128)(2,1)S(1)}, bf16[512,501]{0,1:T(8,128)(2,1)}, u32[]{:S(2)}) copy-start(bf16[512,501]{0,1:T(8,128)(2,1)} %copy-done.1) | copy-start | bytes 1539076
  2889.0 4.2 copy-start.3
  2889.1 4.2 copy-start.4
Sparse Core Ops, SparseCore 0:
  12.6 120.1 all-gather.4
  1523.2 244.8 all-reduce.2
